TPU v7x, 32 devices: a whole 2x2x4 slice. The times are simulated.
32 devices in a mesh: view: 8 (over z, x), slab: 4 (over y, core).
Axes of the slice: x: 2, y: 2, z: 4, core: 2. Of those that a mesh axis runs over, the one named last changes fastest.
Arguments:
- volume: float32 [4, 128, 128], P('slab', 'view'), may hold values from 0 to 2
- tile_blocks: bfloat16 [8, 4, 192, 128, 128], P('view', 'slab'), may hold values from 0.0009994507 to 0.014953613
- pixel_tile: int32 [8, 4, 192], P('view', 'slab'), may hold values from 0 to 127, as said below
- ray_tile: int32 [8, 4, 192], P('view', 'slab'), may hold values from 0 to 127, as said below
- counts: int32 [8, 4], P('view', 'slab'), may hold values from 16 to 192, as said below
- subset_views: int32 [8, 4], P('view'), may hold values from 0 to 7, as said below
- sinogram: float32 [8, 128, 128], P('view', 'slab'), may hold values from 0 to 3
- weights: float32 [8, 128, 128], P('view', 'slab'), may hold values from 0.1 to 1
Outputs:
- updated: float32 [4, 128, 128], P('slab', 'view')
- denominators: float32 [4, 128, 128], P('slab', 'view')
Inputs may be any that keep to these rules, and one draw needn't show every extreme that they name: `counts`: for every group exactly one slab has 192 live slots; every count is at least 16. `pixel_tile`: slots k < 16 of group g name volume tiles g * 16 + k in every slab; slots at or past the count hold indices in range and are unused. `ray_tile`: slots at or past the count hold indices in range and are unused. `subset_views`: each group lists 4 distinct views in rising order.
All inputs are finite; a program needn't handle non-finite values.
Results may differ from a plain program's by a relative error of at most 0.00032.
Values may be sent and summed in bfloat16 or wider, within the bound.
No kernel may reach another device: no remote copies, remote signals or barrier semaphores. Data moves between devices by JAX's collectives and lax.ppermute only.
A program may use at most 64 MiB of HBM per device.

v0:
```python
import jax
import jax.numpy as jnp
from jax import lax
from jax.sharding import PartitionSpec as P

VG = 8
SUBSETS = 2


def make_ratio(totals, measured, weight, subset):
    ray_rows = jnp.arange(totals.shape[0], dtype=jnp.int32)
    view_of = ray_rows % VG
    in_subset = jnp.any(subset[None, :] == view_of[:, None], axis=1).astype(jnp.float32)
    denominator_rays = weight * totals[:, 1]
    residual_rays = in_subset[:, None] * weight * (measured - totals[:, 0])
    return jnp.stack([denominator_rays, residual_rays], axis=1).astype(jnp.bfloat16)


def on_device(volume, tile_blocks, pixel_tile, ray_tile, counts, subset_views, sinogram, weights):
    local_tiles = tile_blocks[0, 0]
    pixel_rows = pixel_tile[0, 0]
    ray_rows = ray_tile[0, 0]
    count_here = counts[0, 0]
    subset = subset_views[0]
    ray_total = sinogram.shape[1] * lax.axis_size("slab")
    voxel_total = volume.shape[1] * lax.axis_size("view")
    live_mask = (jnp.arange(local_tiles.shape[0], dtype=jnp.int32) < count_here).astype(jnp.float32)
    own_image = volume[0].astype(jnp.bfloat16)
    slab_image = lax.all_gather(own_image, "view", axis=0, tiled=True)
    picked = slab_image[pixel_rows]
    operand = jnp.stack([picked, jnp.ones_like(picked)], axis=1)
    products = jnp.einsum("krv,kcv->kcr", local_tiles, operand, preferred_element_type=jnp.float32)
    products = products * live_mask[:, None, None]
    partial_rays = jax.ops.segment_sum(products, ray_rows, num_segments=ray_total)
    measured, weight = (
        lax.all_gather(sinogram[0], "slab", axis=0, tiled=True),
        lax.all_gather(weights[0], "slab", axis=0, tiled=True),
    )
    totals = lax.psum(partial_rays, "slab")
    back_in = make_ratio(totals, measured, weight, subset)
    gathered = back_in[ray_rows]
    back_products = jnp.einsum(
        "krv,kcr->kcv", local_tiles, gathered, preferred_element_type=jnp.float32
    )
    back_products = back_products * live_mask[:, None, None]
    partial_voxels = jax.ops.segment_sum(back_products, pixel_rows, num_segments=voxel_total)
    voxel_share = lax.psum_scatter(partial_voxels, "view", scatter_dimension=0, tiled=True)
    denominators = voxel_share[:, 0, :]
    gradient = voxel_share[:, 1, :]
    updated = jnp.maximum(volume[0] + SUBSETS * gradient / denominators, 0.0)
    return (updated[None], denominators[None])


def solution(mesh):
    return jax.shard_map(
        on_device,
        mesh=mesh,
        in_specs=(
            P("slab", "view", None),
            P("view", "slab", None, None, None),
            P("view", "slab", None),
            P("view", "slab", None),
            P("view", "slab"),
            P("view", None),
            P("view", "slab", None),
            P("view", "slab", None),
        ),
        out_specs=(P("slab", "view", None), P("slab", "view", None)),
        check_vma=False,
    )
```

profile of v0, /device:TPU:0, one launch (start us, length us, event | category | flops | bytes accessed | tf_op | source)
XLA Modules:
  0.0 182.9 jit_solution(6079675270705240020)
XLA Ops:
  7.2 0.0 copy-start.6
  7.2 0.0 copy-start.8
  7.2 0.0 copy-start.4
  7.2 0.0 copy-start.5
  7.2 0.0 all-reduce.5.cloned.1.call-start
  7.9 0.7 convert_element_type.21
  8.6 32.4 %all-gather.1 = bf16[1,128,128]{2,1,0:T(8,128)(2,1)S(1)} all-gather(bf16[1,16,128]{2,1,0:T(8,128)(2,1)S(1)} %convert_element_type.21), channel_id=3, replica_groups=mesh['view'=8,'slab'=4] {'view'}, dimensions={1}, use_global_device_ids=true | all-gather | bytes 36864 | tf_op jit(solution)/shard_map/all_gather | solution.py:29
  41.0 0.7 compare_select_fusion.1
  41.7 0.8 gather_fusion
  42.5 0.1 copy.19
  42.6 0.0 copy-start.7
  42.6 6.1 %fusion.4 = f32[192,2,128]{2,1,0:T(2,128)S(1)} fusion(bf16[1,1,192,128,128]{4,3,2,1,0:T(8,128)(2,1)} %param.9, f32[192]{0:T(256)S(1)} %compare_convert_fusion, bf16[192,1,128]{2,1,0:T(2,128)(2,1)S(1)} %copy.19), kind=kOutput, calls=%fused_computation.8 | convolution fusion | flops 12632064 | bytes 6537984 | tf_op jit(solution)/shard_map/krv,kcv->kcr/dot_general | solution.py:32
  48.7 0.0 copy-start.9
  48.7 0.0 copy-start.2
  48.8 0.0 copy-done.6
  48.8 7.2 %scatter_fusion = f32[128,2,128]{2,1,0:T(2,128)S(1)} fusion(f32[128,2,128]{2,1,0:T(2,128)S(1)} %broadcast.74.clone, s32[192]{0:T(256)S(1)} %bitcast.68, f32[192,2,128]{2,1,0:T(2,128)S(1)} %fusion.4), kind=kCustom, calls=%fused_computation.2 | custom fusion | flops 49152 | bytes 590592 | tf_op jit(solution)/shard_map/scatter-add | solution.py:34
  55.9 0.0 copy-start.1
  56.0 0.6 copy-done.1
  56.6 0.0 all-reduce.5.cloned.1.call-update
  56.6 0.0 all-reduce.7.cloned.1.call-start
  56.7 0.0 copy-done.8
  56.7 0.1 compare_reduce_fusion
  56.8 0.0 copy-done.4
  56.8 5.2 %all-gather = f32[1,128,128]{2,1,0:T(8,128)S(1)} all-gather(f32[1,32,128]{2,1,0:T(8,128)S(1)} %copy-done.4), channel_id=2, replica_groups=mesh['view'=8,'slab'=4] {'slab'}, dimensions={1}, use_global_device_ids=true | all-gather | bytes 81920 | tf_op jit(solution)/shard_map/all_gather | solution.py:37
  62.0 0.0 copy-done.5
  62.1 5.2 %all-gather.2 = f32[1,128,128]{2,1,0:T(8,128)S(1)} all-gather(f32[1,32,128]{2,1,0:T(8,128)S(1)} %copy-done.5), channel_id=4, replica_groups=mesh['view'=8,'slab'=4] {'slab'}, dimensions={1}, use_global_device_ids=true | all-gather | bytes 81920 | tf_op jit(solution)/shard_map/all_gather | solution.py:36
  67.3 22.2 %all-reduce.5.cloned.1.call-done = f32[128,2,128]{2,1,0:T(2,128)} async-done(((f32[128,2,128]{2,1,0:T(2,128)}), f32[128,2,128]{2,1,0:T(2,128)}) %all-reduce.5.cloned.1.call-update) | async-done | bytes 131088 | tf_op jit(solution)/shard_map/psum | solution.py:39
  89.5 1.1 fusion.19
  90.5 0.1 fusion.14
  90.7 0.1 copy.21
  90.7 0.8 gather_fusion.1
  91.6 4.5 %fusion.7 = f32[192,2,128]{2,1,0:T(2,128)S(1)} fusion(bf16[192,2,128]{2,1,0:T(2,128)(2,1)S(1)} %gather_fusion.1, bf16[1,1,192,128,128]{4,3,2,1,0:T(8,128)(2,1)} %param.9, f32[192]{0:T(256)S(1)} %compare_convert_fusion), kind=kOutput, calls=%fused_computation.9 | convolution fusion | flops 12632064 | bytes 6587136 | tf_op jit(solution)/shard_map/krv,kcr->kcv/dot_general | solution.py:42
  96.1 0.0 copy-done.7
  96.2 7.1 %scatter_fusion.1 = f32[128,2,128]{2,1,0:T(2,128)S(1)} fusion(f32[128,2,128]{2,1,0:T(2,128)S(1)} %broadcast.74, s32[192]{0:T(256)S(1)} %bitcast.69, f32[192,2,128]{2,1,0:T(2,128)S(1)} %fusion.7), kind=kCustom, calls=%fused_computation.3 | custom fusion | flops 49152 | bytes 590592 | tf_op jit(solution)/shard_map/scatter-add | solution.py:46
  103.3 0.0 copy-start
  103.3 0.6 copy-done
  104.0 0.0 all-reduce.7.cloned.1.call-update
  104.0 0.0 copy-done.9
  104.0 0.6 dynamic-slice
  105.2 69.4 %all-reduce.7.cloned.1.call-done = f32[128,2,128]{2,1,0:T(2,128)} async-done(((f32[128,2,128]{2,1,0:T(2,128)}), f32[128,2,128]{2,1,0:T(2,128)}) %all-reduce.7.cloned.1.call-update) | async-done | bytes 131088
  174.6 0.8 constant_dynamic-slice_fusion
  175.4 0.0 copy-start.3
  175.5 0.0 copy-done.2
  175.5 0.6 fusion.17
  176.1 0.0 copy-done.3
  (9 shorter events, 0.1 us)
Async XLA Ops:
  7.2 41.6 %copy-start.6 = (s32[1,1,192]{2,1,0:T(1,128)S(1)}, s32[1,1,192]{2,1,0:T(1,128)}, u32[]{:S(2)}) copy-start(s32[1,1,192]{2,1,0:T(1,128)} %param.11) | copy-start | bytes 2308
  7.2 49.5 %copy-start.8 = (s32[1,4]{1,0:T(1,128)S(1)}, s32[1,4]{1,0:T(1,128)}, u32[]{:S(2)}) copy-start(s32[1,4]{1,0:T(1,128)} %param.13) | copy-start | bytes 52
  7.2 49.6 %copy-start.4 = (f32[1,32,128]{2,1,0:T(8,128)S(1)}, f32[1,32,128]{2,1,0:T(8,128)}, u32[]{:S(2)}) copy-start(f32[1,32,128]{2,1,0:T(8,128)} %param.15) | copy-start | bytes 49156
  7.2 54.9 %copy-start.5 = (f32[1,32,128]{2,1,0:T(8,128)S(1)}, f32[1,32,128]{2,1,0:T(8,128)}, u32[]{:S(2)}) copy-start(f32[1,32,128]{2,1,0:T(8,128)} %param.14) | copy-start | bytes 49156
  7.2 82.2 %all-reduce.5.cloned.1.call-start = ((), (), s32[]{:S(2)}) async-start(), calls=%async_computation | async-start | bytes 262144 | tf_op jit(solution)/shard_map/psum | solution.py:39
  42.6 53.6 %copy-start.7 = (s32[1,1,192]{2,1,0:T(1,128)S(1)}, s32[1,1,192]{2,1,0:T(1,128)}, u32[]{:S(2)}) copy-start(s32[1,1,192]{2,1,0:T(1,128)} %param.10) | copy-start | bytes 2308
  48.7 55.3 %copy-start.9 = (u32[32]{0:T(128)S(1)}, u32[32]{0:T(128)}, u32[]{:S(2)}) copy-start(u32[32]{0:T(128)} %constant.40) | copy-start | bytes 388
  48.7 126.7 %copy-start.2 = (f32[1,16,128]{2,1,0:T(8,128)S(1)}, f32[1,16,128]{2,1,0:T(8,128)}, u32[]{:S(2)}) copy-start(f32[1,16,128]{2,1,0:T(8,128)} %param.8) | copy-start | bytes 24580
  55.9 0.7 copy-start.1
  56.6 118.0 %all-reduce.7.cloned.1.call-start = ((), (), s32[]{:S(2)}) async-start(), calls=%async_computation.1 | async-start | bytes 262144
  103.3 0.7 copy-start
  175.4 0.6 copy-start.3
Sparse Core Ops, SparseCore 0:
  56.7 32.6 all-reduce.4
  104.1 70.4 all-reduce.6
where the time goes:
time: 183 us
  waiting for transfers between devices  91.6 us (50%)
  blocking collectives  42.9 us (23%)
  other arithmetic  16.5 us (9%)
  between operations  15.5 us (8%)
  matrix products  10.7 us (6%)
  local copies, waits for them, and re-layouts  5.65 us (3%)
    unnamed x3, waiting for transfers between devices  69.4 us
    all_gather x1, blocking collectives, on_device(): slab_image = lax.all_gather(own_image, 'view', axis=0, tiled=True)  32.4 us
    psum x1, waiting for transfers between devices, on_device(): totals = lax.psum(partial_rays, 'slab')  22.2 us
    scatter-add x1, other arithmetic, on_device(): jax.ops.segment_sum(products, ray_rows, num_segments=ray_total)  7.15 us
    scatter-add x1, other arithmetic, on_device(): jax.ops.segment_sum(back_products, pixel_rows, num_segments=voxel_total)  7.15 us
    dot_general x1, matrix products, on_device(): jnp.einsum('krv,kcv->kcr', local_tiles, operand, preferred_element_type=j...  6.14 us
    all_gather x1, blocking collectives, on_device(): lax.all_gather(sinogram[0], 'slab', axis=0, tiled=True)  5.24 us
    all_gather x1, blocking collectives, on_device(): lax.all_gather(weights[0], 'slab', axis=0, tiled=True)  5.24 us
  transfers between devices with their start and end apart: 2, of which 2 were waited for; matrix products, arithmetic and copies ran while one was open for 0% of the time, Pallas kernels for 0%

commit v1 on v0

--- a/solution.py
+++ b/solution.py
@@ -5,6 +5,7 @@
 
 VG = 8
 SUBSETS = 2
+begin_local_data_up = lambda slab_in: jnp.sum(jax.lax.all_gather(slab_in, axis_name="slab"), 0)
 
 
 def make_ratio(totals, measured, weight, subset):
@@ -36,7 +37,7 @@
         lax.all_gather(sinogram[0], "slab", axis=0, tiled=True),
         lax.all_gather(weights[0], "slab", axis=0, tiled=True),
     )
-    totals = lax.psum(partial_rays, "slab")
+    totals = begin_local_data_up(partial_rays)
     back_in = make_ratio(totals, measured, weight, subset)
     gathered = back_in[ray_rows]
     back_products = jnp.einsum(

time: 183 us -> 168 us (0.918)
  waiting for transfers between devices: 91.6 us -> 69.6 us
  blocking collectives: 42.9 us -> 50.1 us
    psum x1 -> x0, waiting for transfers between devices: 22.2 us -> none  [on_device(): totals = lax.psum(partial_rays, 'slab')]
    all_gather x0 -> x1, blocking collectives: none -> 7.2 us  [jax.lax.all_gather(slab_in, axis_name='slab')]
    unnamed x3 -> x2, waiting for transfers between devices: 69.4 us -> 69.6 us
  transfers between devices with their start and end apart: 2 -> 1, of which waited for: 2 -> 1; matrix products, arithmetic and copies ran while one was open for 0% -> 0% of each run, Pallas kernels for 0% -> 0%
where the time goes in v1:
time: 168 us
  waiting for transfers between devices  69.6 us (41%)
  blocking collectives  50.1 us (30%)
  other arithmetic  17.6 us (10%)
  between operations  15.5 us (9%)
  matrix products  10.6 us (6%)
  local copies, waits for them, and re-layouts  4.07 us (2%)
    unnamed x2, waiting for transfers between devices  69.6 us
    all_gather x1, blocking collectives, on_device(): slab_image = lax.all_gather(own_image, 'view', axis=0, tiled=True)  32.4 us
    all_gather x1, blocking collectives, jax.lax.all_gather(slab_in, axis_name='slab')  7.2 us
    scatter-add x1, other arithmetic, on_device(): jax.ops.segment_sum(products, ray_rows, num_segments=ray_total)  7.15 us
    scatter-add x1, other arithmetic, on_device(): jax.ops.segment_sum(back_products, pixel_rows, num_segments=voxel_total)  7.15 us
    dot_general x1, matrix products, on_device(): jnp.einsum('krv,kcv->kcr', local_tiles, operand, preferred_element_type=j...  6.11 us
    all_gather x1, blocking collectives, on_device(): lax.all_gather(weights[0], 'slab', axis=0, tiled=True)  5.24 us
    all_gather x1, blocking collectives, on_device(): lax.all_gather(sinogram[0], 'slab', axis=0, tiled=True)  5.22 us
  transfers between devices with their start and end apart: 1, of which 1 were waited for; matrix products, arithmetic and copies ran while one was open for 0% of the time, Pallas kernels for 0%

profile of v1, /device:TPU:0, one launch (start us, length us, event | category | flops | bytes accessed | tf_op | source)
XLA Modules:
  0.0 167.5 jit_solution(2142970702210388221)
XLA Ops:
  7.2 0.0 copy-start.5
  7.2 0.0 copy-start.3
  7.2 0.0 copy-start.4
  7.2 0.0 copy-start.7
  7.2 0.0 all-reduce.4.cloned.1.call-start
  7.9 0.7 convert_element_type.21
  8.6 32.4 %all-gather.1 = bf16[1,128,128]{2,1,0:T(8,128)(2,1)S(1)} all-gather(bf16[1,16,128]{2,1,0:T(8,128)(2,1)S(1)} %convert_element_type.21), channel_id=3, replica_groups=mesh['view'=8,'slab'=4] {'view'}, dimensions={1}, use_global_device_ids=true | all-gather | bytes 36864 | tf_op jit(solution)/shard_map/all_gather | solution.py:30
  41.0 0.7 compare_select_fusion.1
  41.7 0.8 gather_fusion
  42.5 0.1 copy.26
  42.6 0.7 compare_select_fusion
  43.3 6.1 %fusion.4 = f32[192,2,128]{2,1,0:T(2,128)S(1)} fusion(bf16[1,1,192,128,128]{4,3,2,1,0:T(8,128)(2,1)} %param.9, f32[192]{0:T(256)S(1)} %compare_convert_fusion, bf16[192,1,128]{2,1,0:T(2,128)(2,1)S(1)} %copy.26), kind=kOutput, calls=%fused_computation.8 | convolution fusion | flops 12632064 | bytes 6537984 | tf_op jit(solution)/shard_map/krv,kcv->kcr/dot_general | solution.py:33
  49.4 0.0 copy-start.6
  49.4 0.0 copy-start.8
  49.4 0.0 copy-start.1
  49.4 0.1 broadcast.74.clone
  49.5 0.0 copy-done.5
  49.5 7.2 %scatter_fusion = f32[128,2,128]{2,1,0:T(2,128)S(1)} fusion(f32[128,2,128]{2,1,0:T(2,128)S(1)} %broadcast.74.clone, s32[192]{0:T(256)S(1)} %bitcast.70, f32[192,2,128]{2,1,0:T(2,128)S(1)} %fusion.4), kind=kCustom, calls=%fused_computation.2 | custom fusion | flops 49152 | bytes 590592 | tf_op jit(solution)/shard_map/scatter-add | solution.py:35
  56.6 7.2 %all-gather.2 = f32[512,2,128]{2,1,0:T(2,128)S(1)} all-gather(f32[128,2,128]{2,1,0:T(2,128)S(1)} %scatter_fusion), channel_id=4, replica_groups=mesh['view'=8,'slab'=4] {'slab'}, dimensions={0}, use_global_device_ids=true | all-gather | bytes 655360 | tf_op jit(solution)/shard_map/all_gather | solution.py:8
  63.8 0.3 reduce_sum.9
  64.1 0.1 fusion.19
  64.2 0.0 copy-done.3
  64.2 5.2 %all-gather = f32[1,128,128]{2,1,0:T(8,128)S(1)} all-gather(f32[1,32,128]{2,1,0:T(8,128)S(1)} %copy-done.3), channel_id=2, replica_groups=mesh['view'=8,'slab'=4] {'slab'}, dimensions={1}, use_global_device_ids=true | all-gather | bytes 81920 | tf_op jit(solution)/shard_map/all_gather | solution.py:38
  69.5 0.0 copy-done.4
  69.5 5.2 %all-gather.3 = f32[1,128,128]{2,1,0:T(8,128)S(1)} all-gather(f32[1,32,128]{2,1,0:T(8,128)S(1)} %copy-done.4), channel_id=5, replica_groups=mesh['view'=8,'slab'=4] {'slab'}, dimensions={1}, use_global_device_ids=true | all-gather | bytes 81920 | tf_op jit(solution)/shard_map/all_gather | solution.py:37
  74.7 0.0 copy-done.7
  74.7 0.1 compare_reduce_fusion
  74.8 0.1 fusion.14
  74.9 0.1 copy.28
  74.9 0.1 copy.29
  75.0 0.2 pad_maximum_fusion
  75.2 0.8 gather_fusion.1
  76.0 4.5 %fusion.7 = f32[192,2,128]{2,1,0:T(2,128)S(1)} fusion(bf16[192,2,128]{2,1,0:T(2,128)(2,1)S(1)} %gather_fusion.1, bf16[1,1,192,128,128]{4,3,2,1,0:T(8,128)(2,1)} %param.9, f32[192]{0:T(256)S(1)} %compare_convert_fusion), kind=kOutput, calls=%fused_computation.9 | convolution fusion | flops 12632064 | bytes 6587136 | tf_op jit(solution)/shard_map/krv,kcr->kcv/dot_general | solution.py:43
  80.6 0.0 copy-done.6
  80.6 7.1 %scatter_fusion.1 = f32[128,2,128]{2,1,0:T(2,128)S(1)} fusion(f32[128,2,128]{2,1,0:T(2,128)S(1)} %broadcast.74, s32[192]{0:T(256)S(1)} %bitcast.71, f32[192,2,128]{2,1,0:T(2,128)S(1)} %fusion.7), kind=kCustom, calls=%fused_computation.3 | custom fusion | flops 49152 | bytes 590592 | tf_op jit(solution)/shard_map/scatter-add | solution.py:47
  87.7 0.0 copy-start
  87.8 0.6 copy-done
  88.4 0.0 all-reduce.4.cloned.1.call-update
  88.4 0.0 copy-done.8
  88.4 0.6 dynamic-slice
  89.7 69.6 %all-reduce.4.cloned.1.call-done = f32[128,2,128]{2,1,0:T(2,128)} async-done(((f32[128,2,128]{2,1,0:T(2,128)}), f32[128,2,128]{2,1,0:T(2,128)}) %all-reduce.4.cloned.1.call-update) | async-done | bytes 131088
  159.2 0.8 constant_dynamic-slice_fusion
  160.1 0.0 copy-start.2
  160.1 0.0 copy-done.1
  160.1 0.6 fusion.17
  160.7 0.0 copy-done.2
  (6 shorter events, 0.1 us)
Async XLA Ops:
  7.2 42.3 %copy-start.5 = (s32[1,1,192]{2,1,0:T(1,128)S(1)}, s32[1,1,192]{2,1,0:T(1,128)}, u32[]{:S(2)}) copy-start(s32[1,1,192]{2,1,0:T(1,128)} %param.11) | copy-start | bytes 2308
  7.2 57.0 %copy-start.3 = (f32[1,32,128]{2,1,0:T(8,128)S(1)}, f32[1,32,128]{2,1,0:T(8,128)}, u32[]{:S(2)}) copy-start(f32[1,32,128]{2,1,0:T(8,128)} %param.15) | copy-start | bytes 49156
  7.2 62.3 %copy-start.4 = (f32[1,32,128]{2,1,0:T(8,128)S(1)}, f32[1,32,128]{2,1,0:T(8,128)}, u32[]{:S(2)}) copy-start(f32[1,32,128]{2,1,0:T(8,128)} %param.14) | copy-start | bytes 49156
  7.2 67.5 %copy-start.7 = (s32[1,4]{1,0:T(1,128)S(1)}, s32[1,4]{1,0:T(1,128)}, u32[]{:S(2)}) copy-start(s32[1,4]{1,0:T(1,128)} %param.13) | copy-start | bytes 52
  7.2 152.0 %all-reduce.4.cloned.1.call-start = ((), (), s32[]{:S(2)}) async-start(), calls=%async_computation | async-start | bytes 262144
  49.4 31.2 %copy-start.6 = (s32[1,1,192]{2,1,0:T(1,128)S(1)}, s32[1,1,192]{2,1,0:T(1,128)}, u32[]{:S(2)}) copy-start(s32[1,1,192]{2,1,0:T(1,128)} %param.10) | copy-start | bytes 2308
  49.4 39.0 %copy-start.8 = (u32[32]{0:T(128)S(1)}, u32[32]{0:T(128)}, u32[]{:S(2)}) copy-start(u32[32]{0:T(128)} %constant.41) | copy-start | bytes 388
  49.4 110.7 %copy-start.1 = (f32[1,16,128]{2,1,0:T(8,128)S(1)}, f32[1,16,128]{2,1,0:T(8,128)}, u32[]{:S(2)}) copy-start(f32[1,16,128]{2,1,0:T(8,128)} %param.8) | copy-start | bytes 24580
  87.7 0.7 copy-start
  160.1 0.6 copy-start.2
Sparse Core Ops, SparseCore 0:
  88.5 70.6 all-reduce.3
